TPU v7x, 32 devices: a whole 2x2x4 slice. The times are simulated.
32 devices in a mesh: rep: 8 (over y, x, core), grp: 4 (over z).
Axes of the slice: x: 2, y: 2, z: 4, core: 2. Of those that a mesh axis runs over, the one named last changes fastest.
Arguments:
- tokens: bfloat16 [16, 1024, 1024], P('rep', 'grp'), may hold values from -6 to 6
- positions: int32 [3, 16, 1024], P(None, 'rep', 'grp'), may hold values from 0 to 15
- ln1_gain: bfloat16 [1024], P('grp'), may hold values from 0.099609375 to 1.8984375
- ln1_bias: bfloat16 [1024], P('grp'), may hold values from -3 to 3
- w_qkv: bfloat16 [1024, 3072], P('grp'), may hold values from -0.1875 to 0.1875
- b_qkv: bfloat16 [3072], P('grp'), may hold values from -3 to 3
- w_out: bfloat16 [1024, 1024], P('grp'), may hold values from -0.75 to 0.75
- b_out: bfloat16 [1024], P('grp'), may hold values from -3 to 3
- ln2_gain: bfloat16 [1024], P('grp'), may hold values from 0.099609375 to 1.8984375
- ln2_bias: bfloat16 [1024], P('grp'), may hold values from -3 to 3
- w_up: bfloat16 [1024, 4096], P('grp'), may hold values from -0.1875 to 0.1875
- b_up: bfloat16 [4096], P('grp'), may hold values from -3 to 3
- w_down: bfloat16 [4096, 1024], P('grp'), may hold values from -0.09375 to 0.09375
- b_down: bfloat16 [1024], P('grp'), may hold values from -3 to 3
- cotangent: bfloat16 [16, 1024, 1024], P('rep', 'grp'), may hold values from -6 to 6
Outputs:
- output: bfloat16 [16, 1024, 1024], P('rep', 'grp')
- grad_tokens: bfloat16 [16, 1024, 1024], P('rep', 'grp')
- grad_ln1_gain: float32 [1024], P('grp')
- grad_ln1_bias: float32 [1024], P('grp')
- grad_w_qkv: float32 [1024, 3072], P('grp')
- grad_b_qkv: float32 [3072], P('grp')
- grad_w_out: float32 [1024, 1024], P('grp')
- grad_b_out: float32 [1024], P('grp')
- grad_ln2_gain: float32 [1024], P('grp')
- grad_ln2_bias: float32 [1024], P('grp')
- grad_w_up: float32 [1024, 4096], P('grp')
- grad_b_up: float32 [4096], P('grp')
- grad_w_down: float32 [4096, 1024], P('grp')
- grad_b_down: float32 [1024], P('grp')
Inputs may be any that keep to these rules, and one draw needn't show every extreme that they name: `positions`: frame, row and column indices of a token.
All inputs are finite; a program needn't handle non-finite values.
Results may differ from a plain program's by a relative error of at most 0.02.
Values may be sent and summed in bfloat16 or wider, within the bound.
A program may use at most 320 MiB of HBM per device.

v0:
```python
import jax
import jax.numpy as jnp
from jax import lax
from jax.sharding import PartitionSpec as P

SCALE = 0.125
EPS = 1e-06


def rotary_angles(positions):
    pair = jnp.arange(32)
    band = (pair >= 10).astype(jnp.int32) + (pair >= 21).astype(jnp.int32)
    start = jnp.where(band == 0, 0, jnp.where(band == 1, 10, 21))
    count = jnp.where(band == 0, 10, 11)
    freq = jnp.power(
        jnp.float32(10000.0), -(pair - start).astype(jnp.float32) / count.astype(jnp.float32)
    )
    pos_f = positions.astype(jnp.float32)
    chosen = jnp.where(
        band[None, :] == 0,
        pos_f[0][:, None],
        jnp.where(band[None, :] == 1, pos_f[1][:, None], pos_f[2][:, None]),
    )
    return chosen * freq[None, :]


def rotate(field, cosine, sine):
    first = field[..., :32]
    second = field[..., 32:]
    return jnp.concatenate(
        [first * cosine - second * sine, first * sine + second * cosine], axis=-1
    )


def normalize(field):
    centred = field - jnp.mean(field, axis=-1, keepdims=True)
    variance = jnp.mean(centred * centred, axis=-1, keepdims=True)
    factor = lax.rsqrt(variance + EPS)
    return (centred * factor, factor)


def norm_back(grad_norm, normed, factor):
    return factor * (
        grad_norm
        - jnp.mean(grad_norm, axis=-1, keepdims=True)
        - normed * jnp.mean(grad_norm * normed, axis=-1, keepdims=True)
    )


def outer(left, right):
    return lax.dot_general(
        left, right, (((0,), (0,)), ((), ())), preferred_element_type=jnp.float32
    )


def back(left, right):
    return lax.dot_general(
        left, right, (((1,), (1,)), ((), ())), preferred_element_type=jnp.float32
    )


def exact_gelu(value):
    return jax.nn.gelu(value, approximate=False)


def column_sum(value):
    return jnp.sum(value.astype(jnp.float32), axis=0)


def forward_pass(params, field_in, positions):
    g1, b1, wqkv, bqkv, wo, bo, g2, b2, w1, bu, w2, bd = params
    field = field_in.astype(jnp.float32)
    count, width = field.shape
    heads = width // 64
    angles = rotary_angles(positions)
    cosine = jnp.cos(angles)[:, None, :]
    sine = jnp.sin(angles)[:, None, :]
    normed1, factor1 = normalize(field)
    h1 = (normed1 * g1.astype(jnp.float32) + b1.astype(jnp.float32)).astype(jnp.bfloat16)
    qkv = jnp.dot(h1, wqkv, preferred_element_type=jnp.float32) + bqkv.astype(jnp.float32)
    query_rot = rotate(qkv[:, :width].reshape(count, heads, 64), cosine, sine).astype(jnp.bfloat16)
    keys_rot = (
        rotate(qkv[:, width : 2 * width].reshape(count, heads, 64), cosine, sine)
        .astype(jnp.bfloat16)
        .reshape(count, width)
    )
    values = qkv[:, 2 * width :].astype(jnp.bfloat16)
    keys_all, values_all = (
        lax.all_gather(keys_rot, "grp", axis=0, tiled=True),
        lax.all_gather(values, "grp", axis=0, tiled=True),
    )
    total = keys_all.shape[0]
    keys_all = keys_all.reshape(total, heads, 64)
    values_all = values_all.reshape(total, heads, 64)
    scores = (
        jnp.einsum("thd,shd->hts", query_rot, keys_all, preferred_element_type=jnp.float32) * SCALE
    )
    top = jnp.max(scores, axis=-1, keepdims=True)
    lse = top + jnp.log(jnp.sum(jnp.exp(scores - top), axis=-1, keepdims=True))
    probs = jnp.exp(scores - lse).astype(jnp.bfloat16)
    mixed = (
        jnp.einsum("hts,shd->thd", probs, values_all, preferred_element_type=jnp.float32)
        .reshape(count, width)
        .astype(jnp.bfloat16)
    )
    second = field + jnp.dot(mixed, wo, preferred_element_type=jnp.float32) + bo.astype(jnp.float32)
    normed2, factor2 = normalize(second)
    h2 = (normed2 * g2.astype(jnp.float32) + b2.astype(jnp.float32)).astype(jnp.bfloat16)
    hidden = jnp.dot(h2, w1, preferred_element_type=jnp.float32) + bu.astype(jnp.float32)
    active = exact_gelu(hidden).astype(jnp.bfloat16)
    result = (
        second + jnp.dot(active, w2, preferred_element_type=jnp.float32) + bd.astype(jnp.float32)
    )
    saved = (
        normed1,
        factor1,
        h1,
        query_rot,
        keys_rot,
        values,
        lse,
        mixed,
        normed2,
        factor2,
        h2,
        hidden,
        active,
        cosine,
        sine,
    )
    return (saved, result.astype(jnp.bfloat16))


def backward_pass(params, saved, grad_in, totals):
    g1, b1, wqkv, bqkv, wo, bo, g2, b2, w1, bu, w2, bd = params
    (
        normed1,
        factor1,
        h1,
        query_rot,
        keys_rot,
        values,
        lse,
        mixed,
        normed2,
        factor2,
        h2,
        hidden,
        active,
        cosine,
        sine,
    ) = saved
    grad_out = grad_in.astype(jnp.float32)
    count, width = grad_out.shape
    heads = width // 64
    grad_y2 = grad_out.astype(jnp.bfloat16)
    grad_w2 = outer(active, grad_y2)
    grad_bd = column_sum(grad_y2)
    grad_act = back(grad_y2, w2)
    unused, pull = jax.vjp(exact_gelu, hidden)
    grad_hidden = pull(grad_act)[0].astype(jnp.bfloat16)
    grad_w1 = outer(h2, grad_hidden)
    grad_bu = column_sum(grad_hidden)
    grad_h2 = back(grad_hidden, w1)
    grad_g2 = jnp.sum(grad_h2 * normed2, axis=0)
    grad_b2 = jnp.sum(grad_h2, axis=0)
    grad_second = grad_out + norm_back(grad_h2 * g2.astype(jnp.float32), normed2, factor2)
    grad_y1 = grad_second.astype(jnp.bfloat16)
    grad_wo = outer(mixed, grad_y1)
    grad_bo = column_sum(grad_y1)
    grad_mixed = back(grad_y1, wo).astype(jnp.bfloat16).reshape(count, heads, 64)
    keys_all, values_all = (
        lax.all_gather(keys_rot, "grp", axis=0, tiled=True),
        lax.all_gather(values, "grp", axis=0, tiled=True),
    )
    total = keys_all.shape[0]
    keys_all = keys_all.reshape(total, heads, 64)
    values_all = values_all.reshape(total, heads, 64)
    scores = (
        jnp.einsum("thd,shd->hts", query_rot, keys_all, preferred_element_type=jnp.float32) * SCALE
    )
    probs = jnp.exp(scores - lse)
    grad_probs = jnp.einsum(
        "thd,shd->hts", grad_mixed, values_all, preferred_element_type=jnp.float32
    )
    delta = jnp.sum(probs * grad_probs, axis=-1, keepdims=True)
    grad_scores = (probs * (grad_probs - delta)).astype(jnp.bfloat16)
    grad_query = (
        jnp.einsum("hts,shd->thd", grad_scores, keys_all, preferred_element_type=jnp.float32)
        * SCALE
    )
    probs_low = probs.astype(jnp.bfloat16)
    grad_values = jnp.einsum(
        "hts,thd->shd", probs_low, grad_mixed, preferred_element_type=jnp.float32
    )
    grad_keys = (
        jnp.einsum("hts,thd->shd", grad_scores, query_rot, preferred_element_type=jnp.float32)
        * SCALE
    )
    keys_own, values_own = (
        lax.psum_scatter(
            grad_keys.reshape(total, width).astype(jnp.bfloat16),
            "grp",
            scatter_dimension=0,
            tiled=True,
        ).astype(jnp.float32),
        lax.psum_scatter(
            grad_values.reshape(total, width).astype(jnp.bfloat16),
            "grp",
            scatter_dimension=0,
            tiled=True,
        ).astype(jnp.float32),
    )
    query_back = rotate(grad_query, cosine, -sine).reshape(count, width)
    keys_back = rotate(keys_own.reshape(count, heads, 64), cosine, -sine).reshape(count, width)
    grad_qkv = jnp.concatenate([query_back, keys_back, values_own], axis=1).astype(jnp.bfloat16)
    grad_wqkv = outer(h1, grad_qkv)
    grad_bqkv = column_sum(grad_qkv)
    grad_h1 = back(grad_qkv, wqkv)
    grad_g1 = jnp.sum(grad_h1 * normed1, axis=0)
    grad_b1 = jnp.sum(grad_h1, axis=0)
    grad_field = grad_second + norm_back(grad_h1 * g1.astype(jnp.float32), normed1, factor1)
    terms = (
        grad_g1,
        grad_b1,
        grad_wqkv,
        grad_bqkv,
        grad_wo,
        grad_bo,
        grad_g2,
        grad_b2,
        grad_w1,
        grad_bu,
        grad_w2,
        grad_bd,
    )
    totals = tuple((a + b for a, b in zip(totals, terms)))
    return (grad_field.astype(jnp.bfloat16), totals)


def local(
    tokens,
    positions,
    ln1_gain,
    ln1_bias,
    w_qkv,
    b_qkv,
    w_out,
    b_out,
    ln2_gain,
    ln2_bias,
    w_up,
    b_up,
    w_down,
    b_down,
    cotangent,
):
    shards = (
        ln1_gain,
        ln1_bias,
        w_qkv,
        b_qkv,
        w_out,
        b_out,
        ln2_gain,
        ln2_bias,
        w_up,
        b_up,
        w_down,
        b_down,
    )
    groups = lax.axis_size("grp")
    totals = tuple((jnp.zeros((s.shape[0] * groups,) + s.shape[1:], jnp.float32) for s in shards))
    outputs = []
    gradients = []
    for index in range(tokens.shape[0]):
        forward_params = (
            lax.all_gather(ln1_gain, "grp", axis=0, tiled=True),
            lax.all_gather(ln1_bias, "grp", axis=0, tiled=True),
            lax.all_gather(w_qkv, "grp", axis=0, tiled=True),
            lax.all_gather(b_qkv, "grp", axis=0, tiled=True),
            lax.all_gather(w_out, "grp", axis=0, tiled=True),
            lax.all_gather(b_out, "grp", axis=0, tiled=True),
            lax.all_gather(ln2_gain, "grp", axis=0, tiled=True),
            lax.all_gather(ln2_bias, "grp", axis=0, tiled=True),
            lax.all_gather(w_up, "grp", axis=0, tiled=True),
            lax.all_gather(b_up, "grp", axis=0, tiled=True),
            lax.all_gather(w_down, "grp", axis=0, tiled=True),
            lax.all_gather(b_down, "grp", axis=0, tiled=True),
        )
        saved, result = forward_pass(forward_params, tokens[index], positions[:, index, :])
        outputs.append(result)
        backward_params = (
            lax.all_gather(ln1_gain, "grp", axis=0, tiled=True),
            lax.all_gather(ln1_bias, "grp", axis=0, tiled=True),
            lax.all_gather(w_qkv, "grp", axis=0, tiled=True),
            lax.all_gather(b_qkv, "grp", axis=0, tiled=True),
            lax.all_gather(w_out, "grp", axis=0, tiled=True),
            lax.all_gather(b_out, "grp", axis=0, tiled=True),
            lax.all_gather(ln2_gain, "grp", axis=0, tiled=True),
            lax.all_gather(ln2_bias, "grp", axis=0, tiled=True),
            lax.all_gather(w_up, "grp", axis=0, tiled=True),
            lax.all_gather(b_up, "grp", axis=0, tiled=True),
            lax.all_gather(w_down, "grp", axis=0, tiled=True),
            lax.all_gather(b_down, "grp", axis=0, tiled=True),
        )
        grad_field, totals = backward_pass(backward_params, saved, cotangent[index], totals)
        gradients.append(grad_field)
    owned = (
        lax.psum_scatter(
            totals[0].astype(jnp.bfloat16), "grp", scatter_dimension=0, tiled=True
        ).astype(jnp.float32),
        lax.psum_scatter(
            totals[1].astype(jnp.bfloat16), "grp", scatter_dimension=0, tiled=True
        ).astype(jnp.float32),
        lax.psum_scatter(
            totals[2].astype(jnp.bfloat16), "grp", scatter_dimension=0, tiled=True
        ).astype(jnp.float32),
        lax.psum_scatter(
            totals[3].astype(jnp.bfloat16), "grp", scatter_dimension=0, tiled=True
        ).astype(jnp.float32),
        lax.psum_scatter(
            totals[4].astype(jnp.bfloat16), "grp", scatter_dimension=0, tiled=True
        ).astype(jnp.float32),
        lax.psum_scatter(
            totals[5].astype(jnp.bfloat16), "grp", scatter_dimension=0, tiled=True
        ).astype(jnp.float32),
        lax.psum_scatter(
            totals[6].astype(jnp.bfloat16), "grp", scatter_dimension=0, tiled=True
        ).astype(jnp.float32),
        lax.psum_scatter(
            totals[7].astype(jnp.bfloat16), "grp", scatter_dimension=0, tiled=True
        ).astype(jnp.float32),
        lax.psum_scatter(
            totals[8].astype(jnp.bfloat16), "grp", scatter_dimension=0, tiled=True
        ).astype(jnp.float32),
        lax.psum_scatter(
            totals[9].astype(jnp.bfloat16), "grp", scatter_dimension=0, tiled=True
        ).astype(jnp.float32),
        lax.psum_scatter(
            totals[10].astype(jnp.bfloat16), "grp", scatter_dimension=0, tiled=True
        ).astype(jnp.float32),
        lax.psum_scatter(
            totals[11].astype(jnp.bfloat16), "grp", scatter_dimension=0, tiled=True
        ).astype(jnp.float32),
    )
    summed = (
        lax.psum(owned[0].astype(jnp.bfloat16), "rep").astype(jnp.float32),
        lax.psum(owned[1].astype(jnp.bfloat16), "rep").astype(jnp.float32),
        lax.psum(owned[2].astype(jnp.bfloat16), "rep").astype(jnp.float32),
        lax.psum(owned[3].astype(jnp.bfloat16), "rep").astype(jnp.float32),
        lax.psum(owned[4].astype(jnp.bfloat16), "rep").astype(jnp.float32),
        lax.psum(owned[5].astype(jnp.bfloat16), "rep").astype(jnp.float32),
        lax.psum(owned[6].astype(jnp.bfloat16), "rep").astype(jnp.float32),
        lax.psum(owned[7].astype(jnp.bfloat16), "rep").astype(jnp.float32),
        lax.psum(owned[8].astype(jnp.bfloat16), "rep").astype(jnp.float32),
        lax.psum(owned[9].astype(jnp.bfloat16), "rep").astype(jnp.float32),
        lax.psum(owned[10].astype(jnp.bfloat16), "rep").astype(jnp.float32),
        lax.psum(owned[11].astype(jnp.bfloat16), "rep").astype(jnp.float32),
    )
    output = jnp.stack(outputs, axis=0)
    grad_tokens = jnp.stack(gradients, axis=0)
    return (
        output,
        grad_tokens,
        summed[0],
        summed[1],
        summed[2],
        summed[3],
        summed[4],
        summed[5],
        summed[6],
        summed[7],
        summed[8],
        summed[9],
        summed[10],
        summed[11],
    )


def solution(mesh):
    placed = (
        P("rep", "grp", None),
        P(None, "rep", "grp"),
        P("grp"),
        P("grp"),
        P("grp", None),
        P("grp"),
        P("grp", None),
        P("grp"),
        P("grp"),
        P("grp"),
        P("grp", None),
        P("grp"),
        P("grp", None),
        P("grp"),
        P("rep", "grp", None),
    )
    return jax.shard_map(
        local,
        mesh=mesh,
        in_specs=placed,
        out_specs=(
            P("rep", "grp", None),
            P("rep", "grp", None),
            P("grp"),
            P("grp"),
            P("grp", None),
            P("grp"),
            P("grp", None),
            P("grp"),
            P("grp"),
            P("grp"),
            P("grp", None),
            P("grp"),
            P("grp", None),
            P("grp"),
        ),
        check_vma=False,
    )
```

profile of v0, /device:TPU:0, one launch (start us, length us, event | category | flops | bytes accessed | tf_op | source)
XLA Modules:
  0.0 1496.7 jit_solution(1610655362138257316)
XLA Ops:
  8.6 14.8 all-gather.2
  24.2 12.4 all-gather.1
  37.3 8.0 all-gather
  50.1 77.6 %all-gather.16.cloned.1.call-done = bf16[1024,3072]{1,0:T(8,128)(2,1)} async-done(((bf16[256,3072]{1,0:T(8,128)(2,1)}), bf16[1024,3072]{1,0:T(8,128)(2,1)}) %all-gather.16.cloned.1.call-update) | async-done | bytes 6291472 | tf_op jit(solution)/shard_map/all_gather | solution.py:280
  157.1 8.3 all-gather.3
  165.4 15.3 %all_gather.43 = bf16[4096]{0:T(1024)(128)(2,1)S(1)} all-gather(bf16[1024]{0:T(1024)(128)(2,1)S(1)} %copy-done.99), channel_id=1, replica_groups=mesh['rep'=8,'grp'=4] {'grp'}, dimensions={0}, use_global_device_ids=true | all-gather | bytes 10240 | tf_op jit(solution)/shard_map/all_gather | solution.py:287
  181.4 11.2 all-gather.5
  192.6 8.3 all-gather.4
  214.4 15.0 %all-gather.28.cloned.1.call-done = bf16[1024,1024]{1,0:T(8,128)(2,1)} async-done(((bf16[256,1024]{1,0:T(8,128)(2,1)}), bf16[1024,1024]{1,0:T(8,128)(2,1)}) %all-gather.28.cloned.1.call-update) | async-done | bytes 2097168 | tf_op jit(solution)/shard_map/all_gather | solution.py:90
  232.3 43.6 %all-gather.18.cloned.1.call-done = bf16[1024,1024]{1,0:T(8,128)(2,1)} async-done(((bf16[256,1024]{1,0:T(8,128)(2,1)}), bf16[1024,1024]{1,0:T(8,128)(2,1)}) %all-gather.18.cloned.1.call-update) | async-done | bytes 2097168 | tf_op jit(solution)/shard_map/all_gather | solution.py:90
  280.5 8.7 convolution_convert_fusion.2
  289.2 32.7 %all-gather.22.cloned.1.call-done = bf16[1024,1024]{1,0:T(8,128)(2,1)} async-done(((bf16[256,1024]{1,0:T(8,128)(2,1)}), bf16[1024,1024]{1,0:T(8,128)(2,1)}) %all-gather.22.cloned.1.call-update) | async-done | bytes 2097168 | tf_op jit(solution)/shard_map/all_gather | solution.py:282
  325.7 43.2 %all-gather.20.cloned.1.call-done = bf16[1024,1024]{0,1:T(8,128)(2,1)} async-done(((bf16[256,1024]{0,1:T(8,128)(2,1)}), bf16[1024,1024]{0,1:T(8,128)(2,1)}) %all-gather.20.cloned.1.call-update) | async-done | bytes 2097168 | tf_op jit(solution)/shard_map/all_gather | solution.py:89
  386.8 131.5 %all-gather.24.cloned.1.call-done = bf16[1024,4096]{1,0:T(8,128)(2,1)} async-done(((bf16[256,4096]{1,0:T(8,128)(2,1)}), bf16[1024,4096]{1,0:T(8,128)(2,1)}) %all-gather.24.cloned.1.call-update) | async-done | bytes 8388624 | tf_op jit(solution)/shard_map/all_gather | solution.py:286
  518.3 17.5 %multiply_convert_fusion.4 = (bf16[256,4096]{1,0:T(8,128)(2,1)}, f32[256,4096]{1,0:T(8,128)}, f32[256,4096]{1,0:T(8,128)}) fusion(f32[4096]{0:T(1024)} %convert_element_type.404, bf16[1024,4096]{1,0:T(8,128)(2,1)} %all-gather.24.cloned.1.call-done, f32[256,1024]{1,0:T(8,128)} %copy-done.16, f32[256]{0:T(256)S(1)} %add_rsqrt_fusion, f32[256]{0:T(256)} %copy-done.89, ...), kind=kOutput, calls=%fused_computation.28 | convolution fusion | flops 2218000384 | bytes 19949568 | tf_op jit(solution)/shard_map/dot_general | solution.py:109
  535.8 16.7 %multiply_convert_fusion.5 = (bf16[256,4096]{1,0:T(8,128)(2,1)}, f32[256,4096]{1,0:T(8,128)}, f32[256,4096]{1,0:T(8,128)}) fusion(f32[4096]{0:T(1024)S(1)} %copy-done.83, bf16[1024,4096]{1,0:T(8,128)(2,1)S(1)} %copy-done.100, f32[256,1024]{1,0:T(8,128)S(1)} %copy-done.11, f32[1024]{0:T(1024)S(1)} %bitcast.273, f32[1024]{0:T(1024)S(1)} %bitcast.267, ...), kind=kOutput, calls=%fused_computation.41 | convolution fusion | flops 2218000384 | bytes 19949568 | tf_op jit(solution)/shard_map/dot_general | solution.py:109
  552.5 115.2 %all-gather.26.cloned.1.call-done = bf16[4096,1024]{1,0:T(8,128)(2,1)} async-done(((bf16[1024,1024]{1,0:T(8,128)(2,1)}), bf16[4096,1024]{1,0:T(8,128)(2,1)}) %all-gather.26.cloned.1.call-update) | async-done | bytes 8388624 | tf_op jit(solution)/shard_map/all_gather | solution.py:288
  667.7 10.3 convert_reduce_fusion
  678.0 6.8 fusion.116
  684.9 11.9 convert_reduce_fusion.1
  696.8 8.0 multiply_reduce_fusion.5
  712.1 15.6 %multiply_reduce_fusion = (f32[16,256]{1,0:T(8,128)}, f32[16,256,1024]{2,1,0:T(8,128)}) fusion(f32[16,256,1024]{2,1,0:T(8,128)} %copy-done, f32[16,256]{1,0:T(8,128)} %copy-done.56, bf16[256,16,64]{0,2,1:T(8,128)(2,1)} %bitcast.234, bf16[1024,16,64]{0,2,1:T(8,128)(2,1)} %bitcast.219), kind=kOutput, calls=%fused_computation.3 | convolution fusion | flops 553644032 | bytes 36208640 | tf_op jit(solution)/shard_map/thd,shd->hts/dot_general | solution.py:183
  729.4 8.1 multiply_convert_fusion
  746.6 16.1 %multiply_reduce_fusion.1 = (f32[16,256]{1,0:T(8,128)}, f32[16,256,1024]{2,1,0:T(8,128)}) fusion(f32[16,256,1024]{2,1,0:T(8,128)} %copy-done.1, f32[16,256]{1,0:T(8,128)} %copy-done.58, bf16[256,16,64]{0,2,1:T(8,128)(2,1)} %bitcast.236, bf16[1024,16,64]{0,2,1:T(8,128)(2,1)} %bitcast.216), kind=kOutput, calls=%fused_computation.5 | convolution fusion | flops 553644032 | bytes 36208640 | tf_op jit(solution)/shard_map/thd,shd->hts/dot_general | solution.py:183
  763.9 8.2 multiply_convert_fusion.1
  776.1 9.4 convolution_convert_fusion.1
  785.6 9.6 convolution_convert_fusion
  799.6 7.9 fusion.14
  807.5 7.1 fusion.15
  815.7 12.9 reduce-scatter.9.cloned.1.call-done
  835.2 38.6 %reduce-scatter.11.cloned.1.call-done = bf16[256,1024]{0,1:T(8,128)(2,1)} async-done(((bf16[1024,1024]{0,1:T(8,128)(2,1)}), bf16[256,1024]{0,1:T(8,128)(2,1)}) %reduce-scatter.11.cloned.1.call-update) | async-done | bytes 524304 | tf_op jit(solution)/shard_map/reduce_scatter | solution.py:207
  873.8 8.0 fusion.100
  881.8 37.5 %reduce-scatter.15.cloned.1.call-done = bf16[256,1024]{0,1:T(8,128)(2,1)} async-done(((bf16[1024,1024]{0,1:T(8,128)(2,1)}), bf16[256,1024]{0,1:T(8,128)(2,1)}) %reduce-scatter.15.cloned.1.call-update) | async-done | bytes 524304 | tf_op jit(solution)/shard_map/reduce_scatter | solution.py:207
  919.4 9.9 add_convert_fusion.2
  929.9 10.1 fusion.107
  940.0 11.8 add_convert_fusion.1
  951.9 10.0 fusion.67
  961.9 12.3 add_convert_fusion
  974.8 11.6 all-gather.6
  989.0 6.8 fusion.36
  995.9 5.8 fusion.37
  1002.9 73.8 %reduce-scatter.17.cloned.1.call-done = bf16[256,3072]{1,0:T(8,128)(2,1)} async-done(((bf16[1024,3072]{1,0:T(8,128)(2,1)}), bf16[256,3072]{1,0:T(8,128)(2,1)}) %reduce-scatter.17.cloned.1.call-update) | async-done | bytes 1572880 | tf_op jit(solution)/shard_map/reduce_scatter | solution.py:316
  1076.7 147.4 %reduce-scatter.21.cloned.1.call-done = bf16[256,4096]{1,0:T(8,128)(2,1)} async-done(((bf16[1024,4096]{1,0:T(8,128)(2,1)}), bf16[256,4096]{1,0:T(8,128)(2,1)}) %reduce-scatter.21.cloned.1.call-update) | async-done | bytes 2097168 | tf_op jit(solution)/shard_map/reduce_scatter | solution.py:334
  1224.1 147.5 %reduce-scatter.23.cloned.1.call-done = bf16[1024,1024]{1,0:T(8,128)(2,1)} async-done(((bf16[4096,1024]{1,0:T(8,128)(2,1)}), bf16[1024,1024]{1,0:T(8,128)(2,1)}) %reduce-scatter.23.cloned.1.call-update) | async-done | bytes 2097168 | tf_op jit(solution)/shard_map/reduce_scatter | solution.py:340
  1377.7 6.3 fusion.58
  1384.1 18.4 %all-reduce.10 = (bf16[1024]{0:T(1024)(128)(2,1)S(1)}, bf16[1024]{0:T(1024)(128)(2,1)S(1)}, bf16[3072]{0:T(1024)(128)(2,1)S(1)}, bf16[1024]{0:T(1024)(128)(2,1)S...) all-reduce(bf16[1024]{0:T(1024)(128)(2,1)S(1)} %add_convert_fusion., ...), channel_id=6, replica_groups=mesh['rep'=8,'grp'=4] {'grp'}, use_global_device_ids=true, to_apply=%region_28.29.clone | all-reduce | flops 13312 | bytes 53248
  1403.0 12.3 all-reduce.8
  1423.3 56.7 %all-reduce.13.cloned.1.call-done = (bf16[256,3072]{1,0:T(8,128)(2,1)}, bf16[256,1024]{1,0:T(8,128)(2,1)}, bf16[256,4096]{1,0:T(8,128)(2,1)}, bf16[1024,1024]{1,0:T(8,128)(2,1)}) async-done(((bf16[256,3072]{1,0:T(8,128)(2,1)}, bf16[256,1024]{1,0:T(8,128)(2,1)}, bf16[256,4096]{1,0:T(8,128)(2,1)}, bf16[1024,1024]{1,0:T(8,128)(2,1)}), (bf16[256,3072]{1,0:T(8,128)(2,1)}, bf16[256,1024]{1,0:T(8,128)(2,1)}, ...) | async-done | bytes 6291472 | tf_op jit(solution)/shard_map/psum | solution.py:350
  (385 shorter events, 141.9 us)
Async XLA Ops:
  7.2 120.6 %all-gather.16.cloned.1.call-start = ((), (), s32[]{:S(2)}) async-start(), calls=%async_computation.8 | async-start | bytes 7864320 | tf_op jit(solution)/shard_map/all_gather | solution.py:280
  7.9 193.0 %all-gather.30.cloned.1.call-start = ((), (), s32[]{:S(2)}) async-start(), calls=%async_computation.15 | async-start | bytes 2621440 | tf_op jit(solution)/shard_map/all_gather | solution.py:89
  23.5 109.2 %copy-start.92 = (f32[4,1,768]{2,1,0:T(1,128)}, f32[4,1,768]{2,1,0:T(1,128)S(1)}, u32[]{:S(2)}) copy-start(f32[4,1,768]{2,1,0:T(1,128)S(1)} %convert_element_type.476) | copy-start | bytes 36868
  36.6 104.3 %copy-start.54 = (f32[4,1,256]{2,1,0:T(1,128)}, f32[4,1,256]{2,1,0:T(1,128)S(1)}, u32[]{:S(2)}) copy-start(f32[4,1,256]{2,1,0:T(1,128)S(1)} %convert_element_type.475) | copy-start | bytes 12292
  45.3 95.6 %copy-start.51 = (f32[4,1,256]{2,1,0:T(1,128)}, f32[4,1,256]{2,1,0:T(1,128)S(1)}, u32[]{:S(2)}) copy-start(f32[4,1,256]{2,1,0:T(1,128)S(1)} %convert_element_type.474) | copy-start | bytes 12292
  46.7 85.9 %copy-start.71 = (f32[256]{0:T(256)}, f32[256]{0:T(256)S(1)}, u32[]{:S(2)}) copy-start(f32[256]{0:T(256)S(1)} %get-tuple-element.143) | copy-start | bytes 3076
  46.8 94.1 %copy-start.66 = (f32[256]{0:T(256)}, f32[256]{0:T(256)S(1)}, u32[]{:S(2)}) copy-start(f32[256]{0:T(256)S(1)} %get-tuple-element.144) | copy-start | bytes 3076
  48.4 84.3 %copy-start.86 = (f32[256]{0:T(256)}, f32[256]{0:T(256)S(1)}, u32[]{:S(2)}) copy-start(f32[256]{0:T(256)S(1)} %add_rsqrt_fusion.1) | copy-start | bytes 3076
  50.1 86.6 %copy-start.62 = (f32[256,32]{0,1:T(8,128)}, f32[256,32]{0,1:T(8,128)S(1)}, u32[]{:S(2)}) copy-start(f32[256,32]{0,1:T(8,128)S(1)} %get-tuple-element.121) | copy-start | bytes 98308
  50.1 103.4 %copy-start.60 = (f32[256,32]{0,1:T(8,128)}, f32[256,32]{0,1:T(8,128)S(1)}, u32[]{:S(2)}) copy-start(f32[256,32]{0,1:T(8,128)S(1)} %get-tuple-element.106) | copy-start | bytes 98308
  137.7 63.2 %copy-start.32 = (bf16[256,16,32]{0,2,1:T(8,128)(2,1)}, bf16[256,16,32]{0,2,1:T(8,128)(2,1)S(1)}, u32[]{:S(2)}) copy-start(bf16[256,16,32]{0,2,1:T(8,128)(2,1)S(1)} %get-tuple-element.82) | copy-start | bytes 786436
  138.6 90.8 %all-gather.28.cloned.1.call-start = ((), (), s32[]{:S(2)}) async-start(), calls=%async_computation.14 | async-start | bytes 2621440 | tf_op jit(solution)/shard_map/all_gather | solution.py:90
  140.8 135.1 %all-gather.18.cloned.1.call-start = ((), (), s32[]{:S(2)}) async-start(), calls=%async_computation.9 | async-start | bytes 2621440 | tf_op jit(solution)/shard_map/all_gather | solution.py:90
  148.3 173.6 %all-gather.22.cloned.1.call-start = ((), (), s32[]{:S(2)}) async-start(), calls=%async_computation.11 | async-start | bytes 2621440 | tf_op jit(solution)/shard_map/all_gather | solution.py:282
  148.9 220.0 %all-gather.20.cloned.1.call-start = ((), (), s32[]{:S(2)}) async-start(), calls=%async_computation.10 | async-start | bytes 2621440 | tf_op jit(solution)/shard_map/all_gather | solution.py:89
  153.6 27.8 %copy-start.102 = (bf16[256]{0:T(256)(128)(2,1)S(1)}, bf16[256]{0:T(256)(128)(2,1)}, u32[]{:S(2)}) copy-start(bf16[256]{0:T(256)(128)(2,1)} %param.24) | copy-start | bytes 1540
  153.6 39.0 %copy-start.103 = (bf16[256]{0:T(256)(128)(2,1)S(1)}, bf16[256]{0:T(256)(128)(2,1)}, u32[]{:S(2)}) copy-start(bf16[256]{0:T(256)(128)(2,1)} %param.23) | copy-start | bytes 1540
  154.7 46.2 %copy-start.34 = (bf16[256,16,32]{0,2,1:T(8,128)(2,1)S(1)}, bf16[256,16,32]{0,2,1:T(8,128)(2,1)}, u32[]{:S(2)}) copy-start(bf16[256,16,32]{0,2,1:T(8,128)(2,1)} %get-tuple-element.83) | copy-start | bytes 786436
  155.6 362.8 %all-gather.24.cloned.1.call-start = ((), (), s32[]{:S(2)}) async-start(), calls=%async_computation.12 | async-start | bytes 10485760 | tf_op jit(solution)/shard_map/all_gather | solution.py:286
  156.3 511.4 %all-gather.26.cloned.1.call-start = ((), (), s32[]{:S(2)}) async-start(), calls=%async_computation.13 | async-start | bytes 10485760 | tf_op jit(solution)/shard_map/all_gather | solution.py:288
  157.1 657.5 %reduce-scatter.13.cloned.1.call-start = ((), (), s32[]{:S(2)}) async-start(), calls=%async_computation.18 | async-start | bytes 2621440 | tf_op jit(solution)/shard_map/reduce_scatter | solution.py:201
  232.3 56.9 %copy-start.9 = (bf16[1024,1024]{0,1:T(8,128)(2,1)}, bf16[1024,1024]{0,1:T(8,128)(2,1)S(1)}, u32[]{:S(2)}) copy-start(bf16[1024,1024]{0,1:T(8,128)(2,1)S(1)} %copy.56) | copy-start | bytes 6291460
  289.2 79.8 %copy-start.36 = (bf16[256,16,32]{0,2,1:T(8,128)(2,1)S(1)}, bf16[256,16,32]{0,2,1:T(8,128)(2,1)}, u32[]{:S(2)}) copy-start(bf16[256,16,32]{0,2,1:T(8,128)(2,1)} %get-tuple-element.78) | copy-start | bytes 786436
  321.8 47.1 %copy-start.38 = (bf16[256,16,32]{0,2,1:T(8,128)(2,1)S(1)}, bf16[256,16,32]{0,2,1:T(8,128)(2,1)}, u32[]{:S(2)}) copy-start(bf16[256,16,32]{0,2,1:T(8,128)(2,1)} %get-tuple-element.79) | copy-start | bytes 786436
  324.5 44.4 %copy-start.89 = (f32[256]{0:T(256)}, f32[256]{0:T(256)S(1)}, u32[]{:S(2)}) copy-start(f32[256]{0:T(256)S(1)} %broadcast_multiply_fusion.8) | copy-start | bytes 3076
  385.5 319.4 %copy-start.69 = (f32[256]{0:T(256)}, f32[256]{0:T(256)S(1)}, u32[]{:S(2)}) copy-start(f32[256]{0:T(256)S(1)} %broadcast_multiply_fusion.10) | copy-start | bytes 3076
  386.7 318.1 %copy-start.93 = (f32[256]{0:T(256)}, f32[256]{0:T(256)S(1)}, u32[]{:S(2)}) copy-start(f32[256]{0:T(256)S(1)} %add_rsqrt_fusion) | copy-start | bytes 3076
  386.8 318.1 %copy-start.77 = (f32[256]{0:T(256)}, f32[256]{0:T(256)S(1)}, u32[]{:S(2)}) copy-start(f32[256]{0:T(256)S(1)} %add_rsqrt_fusion.2) | copy-start | bytes 3076
  741.7 86.9 %reduce-scatter.9.cloned.1.call-start = ((), (), s32[]{:S(2)}) async-start(), calls=%async_computation.16 | async-start | bytes 2621440 | tf_op jit(solution)/shard_map/reduce_scatter | solution.py:201
  776.0 97.7 %reduce-scatter.11.cloned.1.call-start = ((), (), s32[]{:S(2)}) async-start(), calls=%async_computation.17 | async-start | bytes 2621440 | tf_op jit(solution)/shard_map/reduce_scatter | solution.py:207
  785.6 133.8 %reduce-scatter.15.cloned.1.call-start = ((), (), s32[]{:S(2)}) async-start(), calls=%async_computation.19 | async-start | bytes 2621440 | tf_op jit(solution)/shard_map/reduce_scatter | solution.py:207
  795.3 207.6 %reduce-scatter.19.cloned.1.call-start = ((), (), s32[]{:S(2)}) async-start(), calls=%async_computation.21 | async-start | bytes 2621440 | tf_op jit(solution)/shard_map/reduce_scatter | solution.py:322
  799.4 277.4 %reduce-scatter.17.cloned.1.call-start = ((), (), s32[]{:S(2)}) async-start(), calls=%async_computation.20 | async-start | bytes 7864320 | tf_op jit(solution)/shard_map/reduce_scatter | solution.py:316
  807.5 22.4 %copy-start.63 = (f32[256,32]{0,1:T(8,128)S(1)}, f32[256,32]{0,1:T(8,128)}, u32[]{:S(2)}) copy-start(f32[256,32]{0,1:T(8,128)} %copy-done.62) | copy-start | bytes 98308
  807.5 22.4 %copy-start.65 = (f32[256,32]{0,1:T(8,128)S(1)}, f32[256,32]{0,1:T(8,128)}, u32[]{:S(2)}) copy-start(f32[256,32]{0,1:T(8,128)} %get-tuple-element.122) | copy-start | bytes 98308
  831.4 42.4 %copy-start.7 = (bf16[2,256,1024]{2,1,0:T(8,128)(2,1)S(1)}, bf16[2,256,1024]{2,1,0:T(8,128)(2,1)}, u32[]{:S(2)}) copy-start(bf16[2,256,1024]{2,1,0:T(8,128)(2,1)} %param.15) | copy-start | bytes 3145732
  831.4 42.4 %copy-start.52 = (f32[4,1,256]{2,1,0:T(1,128)S(1)}, f32[4,1,256]{2,1,0:T(1,128)}, u32[]{:S(2)}) copy-start(f32[4,1,256]{2,1,0:T(1,128)} %copy-done.51) | copy-start | bytes 12292
  831.4 42.4 %copy-start.55 = (f32[4,1,256]{2,1,0:T(1,128)S(1)}, f32[4,1,256]{2,1,0:T(1,128)}, u32[]{:S(2)}) copy-start(f32[4,1,256]{2,1,0:T(1,128)} %copy-done.54) | copy-start | bytes 12292
  831.4 42.4 %copy-start.67 = (f32[256]{0:T(256)S(1)}, f32[256]{0:T(256)}, u32[]{:S(2)}) copy-start(f32[256]{0:T(256)} %copy-done.66) | copy-start | bytes 3076
  831.4 42.4 %copy-start.75 = (f32[256]{0:T(256)S(1)}, f32[256]{0:T(256)}, u32[]{:S(2)}) copy-start(f32[256]{0:T(256)} %copy-done.74) | copy-start | bytes 3076
  873.8 45.6 %copy-start.72 = (f32[256]{0:T(256)S(1)}, f32[256]{0:T(256)}, u32[]{:S(2)}) copy-start(f32[256]{0:T(256)} %copy-done.71) | copy-start | bytes 3076
  873.8 45.5 %copy-start.87 = (f32[256]{0:T(256)S(1)}, f32[256]{0:T(256)}, u32[]{:S(2)}) copy-start(f32[256]{0:T(256)} %copy-done.86) | copy-start | bytes 3076
  929.3 294.8 %reduce-scatter.21.cloned.1.call-start = ((), (), s32[]{:S(2)}) async-start(), calls=%async_computation.22 | async-start | bytes 10485760 | tf_op jit(solution)/shard_map/reduce_scatter | solution.py:334
  951.8 419.8 %reduce-scatter.23.cloned.1.call-start = ((), (), s32[]{:S(2)}) async-start(), calls=%async_computation.23 | async-start | bytes 10485760 | tf_op jit(solution)/shard_map/reduce_scatter | solution.py:340
  974.2 505.9 %all-reduce.13.cloned.1.call-start = ((), (), s32[]{:S(2)}) async-start(), calls=%async_computation.24 | async-start | bytes 12582912 | tf_op jit(solution)/shard_map/psum | solution.py:350
  1001.7 369.9 %copy-start.21 = (bf16[256,16,64]{0,2,1:T(8,128)(2,1)S(1)}, bf16[256,16,64]{0,2,1:T(8,128)(2,1)}, u32[]{:S(2)}) copy-start(bf16[256,16,64]{0,2,1:T(8,128)(2,1)} %pad_maximum_fusion.11) | copy-start | bytes 1572868
  1001.7 369.9 %copy-start.22 = (bf16[256,16,64]{0,2,1:T(8,128)(2,1)S(1)}, bf16[256,16,64]{0,2,1:T(8,128)(2,1)}, u32[]{:S(2)}) copy-start(bf16[256,16,64]{0,2,1:T(8,128)(2,1)} %pad_maximum_fusion.10) | copy-start | bytes 1572868
  1377.7 42.3 %copy-start.15 = (f32[256,1024]{1,0:T(8,128)S(1)}, f32[256,1024]{1,0:T(8,128)}, u32[]{:S(2)}) copy-start(f32[256,1024]{1,0:T(8,128)} %get-tuple-element.93) | copy-start | bytes 3145732
  (84 other events, 655.6 us)
Sparse Core Ops, SparseCore 0:
  9.6 118.1 all-gather.15
  138.8 44.5 all-gather.29
  185.5 43.8 all-gather.27
  231.4 44.4 all-gather.17
  277.3 44.4 all-gather.21
  323.8 45.0 all-gather.19
  370.5 147.7 all-gather.23
  519.9 147.7 all-gather.25
  741.8 41.7 reduce-scatter.12
  785.8 42.8 reduce-scatter.8
  830.9 42.8 reduce-scatter.10
  876.5 42.8 reduce-scatter.14
  921.6 42.8 reduce-scatter.18
  966.7 110.0 reduce-scatter.16
  1078.9 145.1 reduce-scatter.20
  1226.3 145.2 reduce-scatter.22
  1375.0 104.9 all-reduce.12
where the time goes:
time: 1500 us
  waiting for transfers between devices  976 us (65%)
  matrix products  271 us (18%)
  blocking collectives  121 us (8%)
  other arithmetic  63.2 us (4%)
  local copies, waits for them, and re-layouts  46.6 us (3%)
  between operations  17.9 us (1%)
    reduce_scatter x1, waiting for transfers between devices, local(): lax.psum_scatter(totals[10].astype(jnp.bfloat16), 'grp', scatter_dimensio...  147 us
    reduce_scatter x1, waiting for transfers between devices, local(): lax.psum_scatter(totals[8].astype(jnp.bfloat16), 'grp', scatter_dimension...  147 us
    all_gather x1, waiting for transfers between devices, local(): lax.all_gather(w_up, 'grp', axis=0, tiled=True)  132 us
    all_gather x1, waiting for transfers between devices, local(): lax.all_gather(w_down, 'grp', axis=0, tiled=True)  115 us
    all_gather x1, waiting for transfers between devices, local(): lax.all_gather(w_qkv, 'grp', axis=0, tiled=True)  77.6 us
    reduce_scatter x2, waiting for transfers between devices, backward_pass(): lax.psum_scatter(grad_values.reshape(total, width).astype(jnp.bfloat16),...  76.1 us
    reduce_scatter x1, waiting for transfers between devices, local(): lax.psum_scatter(totals[2].astype(jnp.bfloat16), 'grp', scatter_dimension...  73.8 us
    dot_general x8, matrix products, outer(): lax.dot_general(left, right, (((0,), (0,)), ((), ())), preferred_element_...  65.9 us
  transfers between devices with their start and end apart: 17, of which 14 were waited for; matrix products, arithmetic and copies ran while one was open for 18% of the time, Pallas kernels for 0%

commit v1 on v0

--- a/solution.py
+++ b/solution.py
@@ -347,7 +347,7 @@
     summed = (
         lax.psum(owned[0].astype(jnp.bfloat16), "rep").astype(jnp.float32),
         lax.psum(owned[1].astype(jnp.bfloat16), "rep").astype(jnp.float32),
-        lax.psum(owned[2].astype(jnp.bfloat16), "rep").astype(jnp.float32),
+        jnp.sum(lax.all_gather(owned[2].astype(jnp.bfloat16), "rep"), axis=0).astype(jnp.float32),
         lax.psum(owned[3].astype(jnp.bfloat16), "rep").astype(jnp.float32),
         lax.psum(owned[4].astype(jnp.bfloat16), "rep").astype(jnp.float32),
         lax.psum(owned[5].astype(jnp.bfloat16), "rep").astype(jnp.float32),

time: 1500 us -> 1560 us (1.040)
  waiting for transfers between devices: 976 us -> 1030 us
    all_gather x0 -> x1, waiting for transfers between devices: none -> 65 us  [local(): lax.all_gather(owned[2].astype(jnp.bfloat16), 'rep')]
    reduce_scatter x1, waiting for transfers between devices: 73.8 us -> 114 us  [local(): lax.psum_scatter(totals[2].astype(jnp.bfloat16), 'grp', scatter_dimension...]
    psum x1, waiting for transfers between devices: 56.7 us -> 19.7 us  [local(): lax.psum(owned[4].astype(jnp.bfloat16), 'rep').astype(jnp.float32)]
    reduce_scatter x1, waiting for transfers between devices: 0.02 us -> 35.2 us  [local(): lax.psum_scatter(totals[4].astype(jnp.bfloat16), 'grp', scatter_dimension...]
    reduce_scatter x2, waiting for transfers between devices: 76.1 us -> 43.5 us  [backward_pass(): lax.psum_scatter(grad_values.reshape(total, width).astype(jnp.bfloat16),...]
  transfers between devices with their start and end apart: 17 -> 18, of which waited for: 14 -> 15; matrix products, arithmetic and copies ran while one was open for 18% -> 18% of each run, Pallas kernels for 0% -> 0%
where the time goes in v1:
time: 1560 us; the launch traced here: 1550 us
  waiting for transfers between devices  1030 us (66%)
  matrix products  265 us (17%)
  blocking collectives  118 us (8%)
  other arithmetic  71.9 us (5%)
  local copies, waits for them, and re-layouts  46.8 us (3%)
  between operations  18.3 us (1%)
    reduce_scatter x1, waiting for transfers between devices, local(): lax.psum_scatter(totals[10].astype(jnp.bfloat16), 'grp', scatter_dimensio...  147 us
    reduce_scatter x1, waiting for transfers between devices, local(): lax.psum_scatter(totals[8].astype(jnp.bfloat16), 'grp', scatter_dimension...  146 us
    all_gather x1, waiting for transfers between devices, local(): lax.all_gather(w_up, 'grp', axis=0, tiled=True)  132 us
    all_gather x1, waiting for transfers between devices, local(): lax.all_gather(w_down, 'grp', axis=0, tiled=True)  116 us
    reduce_scatter x1, waiting for transfers between devices, local(): lax.psum_scatter(totals[2].astype(jnp.bfloat16), 'grp', scatter_dimension...  114 us
    all_gather x1, waiting for transfers between devices, local(): lax.all_gather(w_qkv, 'grp', axis=0, tiled=True)  77.6 us
    dot_general x8, matrix products, outer(): lax.dot_general(left, right, (((0,), (0,)), ((), ())), preferred_element_...  65.6 us
    all_gather x1, waiting for transfers between devices, local(): lax.all_gather(owned[2].astype(jnp.bfloat16), 'rep')  65 us
  transfers between devices with their start and end apart: 18, of which 15 were waited for; matrix products, arithmetic and copies ran while one was open for 18% of the time, Pallas kernels for 0%

profile of v1, /device:TPU:0, one launch (start us, length us, event | category | flops | bytes accessed | tf_op | source)
XLA Modules:
  0.0 1553.2 jit_solution(17400942665134071687)
XLA Ops:
  8.6 14.8 all-gather.3
  24.2 12.4 all-gather.2
  37.3 8.0 all-gather.1
  50.2 77.6 %all-gather.18.cloned.1.call-done = bf16[1024,3072]{1,0:T(8,128)(2,1)} async-done(((bf16[256,3072]{1,0:T(8,128)(2,1)}), bf16[1024,3072]{1,0:T(8,128)(2,1)}) %all-gather.18.cloned.1.call-update) | async-done | bytes 6291472 | tf_op jit(solution)/shard_map/all_gather | solution.py:280
  157.1 8.3 all-gather.4
  165.4 15.3 all_gather.93
  181.3 11.2 all-gather.6
  192.6 8.3 all-gather.5
  214.4 15.0 all-gather.30.cloned.1.call-done
  232.3 43.6 %all-gather.20.cloned.1.call-done = bf16[1024,1024]{1,0:T(8,128)(2,1)} async-done(((bf16[256,1024]{1,0:T(8,128)(2,1)}), bf16[1024,1024]{1,0:T(8,128)(2,1)}) %all-gather.20.cloned.1.call-update) | async-done | bytes 2097168 | tf_op jit(solution)/shard_map/all_gather | solution.py:90
  280.5 8.7 convolution_convert_fusion.2
  289.2 32.7 %all-gather.24.cloned.1.call-done = bf16[1024,1024]{1,0:T(8,128)(2,1)} async-done(((bf16[256,1024]{1,0:T(8,128)(2,1)}), bf16[1024,1024]{1,0:T(8,128)(2,1)}) %all-gather.24.cloned.1.call-update) | async-done | bytes 2097168 | tf_op jit(solution)/shard_map/all_gather | solution.py:282
  325.7 43.2 %all-gather.22.cloned.1.call-done = bf16[1024,1024]{0,1:T(8,128)(2,1)} async-done(((bf16[256,1024]{0,1:T(8,128)(2,1)}), bf16[1024,1024]{0,1:T(8,128)(2,1)}) %all-gather.22.cloned.1.call-update) | async-done | bytes 2097168 | tf_op jit(solution)/shard_map/all_gather | solution.py:89
  386.8 131.5 %all-gather.26.cloned.1.call-done = bf16[1024,4096]{1,0:T(8,128)(2,1)} async-done(((bf16[256,4096]{1,0:T(8,128)(2,1)}), bf16[1024,4096]{1,0:T(8,128)(2,1)}) %all-gather.26.cloned.1.call-update) | async-done | bytes 8388624 | tf_op jit(solution)/shard_map/all_gather | solution.py:286
  518.3 17.1 %multiply_convert_fusion.4 = (bf16[256,4096]{1,0:T(8,128)(2,1)}, f32[256,4096]{1,0:T(8,128)}, f32[256,4096]{1,0:T(8,128)}) fusion(f32[4096]{0:T(1024)} %convert_element_type.406, bf16[1024,4096]{1,0:T(8,128)(2,1)} %all-gather.26.cloned.1.call-done, f32[256,1024]{1,0:T(8,128)} %copy-done.16, f32[256]{0:T(256)S(1)} %add_rsqrt_fusion, f32[256]{0:T(256)} %copy-done.83, ...), kind=kOutput, calls=%fused_computation.28 | convolution fusion | flops 2218000384 | bytes 19949568 | tf_op jit(solution)/shard_map/dot_general | solution.py:109
  535.4 16.7 %multiply_convert_fusion.5 = (bf16[256,4096]{1,0:T(8,128)(2,1)}, f32[256,4096]{1,0:T(8,128)}, f32[256,4096]{1,0:T(8,128)}) fusion(f32[4096]{0:T(1024)S(1)} %copy-done.77, bf16[1024,4096]{1,0:T(8,128)(2,1)S(1)} %copy-done.94, f32[256,1024]{1,0:T(8,128)S(1)} %copy-done.11, f32[1024]{0:T(1024)S(1)} %bitcast.275, f32[1024]{0:T(1024)S(1)} %bitcast.269, ...), kind=kOutput, calls=%fused_computation.41 | convolution fusion | flops 2218000384 | bytes 19949568 | tf_op jit(solution)/shard_map/dot_general | solution.py:109
  552.1 115.6 %all-gather.28.cloned.1.call-done = bf16[4096,1024]{1,0:T(8,128)(2,1)} async-done(((bf16[1024,1024]{1,0:T(8,128)(2,1)}), bf16[4096,1024]{1,0:T(8,128)(2,1)}) %all-gather.28.cloned.1.call-update) | async-done | bytes 8388624 | tf_op jit(solution)/shard_map/all_gather | solution.py:288
  667.7 10.3 convert_reduce_fusion
  678.0 6.8 fusion.116
  684.9 11.9 convert_reduce_fusion.1
  696.8 8.0 multiply_reduce_fusion.5
  712.1 15.6 %multiply_reduce_fusion = (f32[16,256]{1,0:T(8,128)}, f32[16,256,1024]{2,1,0:T(8,128)}) fusion(f32[16,256,1024]{2,1,0:T(8,128)} %copy-done, f32[16,256]{1,0:T(8,128)} %copy-done.54, bf16[256,16,64]{0,2,1:T(8,128)(2,1)} %bitcast.236, bf16[1024,16,64]{0,2,1:T(8,128)(2,1)} %bitcast.220), kind=kOutput, calls=%fused_computation.3 | convolution fusion | flops 553644032 | bytes 36208640 | tf_op jit(solution)/shard_map/thd,shd->hts/dot_general | solution.py:183
  729.3 8.1 multiply_convert_fusion
  746.5 16.1 %multiply_reduce_fusion.1 = (f32[16,256]{1,0:T(8,128)}, f32[16,256,1024]{2,1,0:T(8,128)}) fusion(f32[16,256,1024]{2,1,0:T(8,128)} %copy-done.1, f32[16,256]{1,0:T(8,128)} %copy-done.56, bf16[256,16,64]{0,2,1:T(8,128)(2,1)} %bitcast.238, bf16[1024,16,64]{0,2,1:T(8,128)(2,1)} %bitcast.217), kind=kOutput, calls=%fused_computation.5 | convolution fusion | flops 553644032 | bytes 36208640 | tf_op jit(solution)/shard_map/thd,shd->hts/dot_general | solution.py:183
  763.8 8.2 multiply_convert_fusion.1
  776.2 9.4 convolution_convert_fusion.1
  785.6 9.6 convolution_convert_fusion
  799.7 10.1 fusion.107
  809.9 11.7 add_convert_fusion.1
  822.8 9.9 fusion.67
  832.8 12.0 add_convert_fusion
  845.0 7.9 fusion.14
  852.9 7.1 fusion.15
  873.8 8.0 fusion.100
  881.8 37.5 %reduce-scatter.15.cloned.1.call-done = bf16[256,1024]{0,1:T(8,128)(2,1)} async-done(((bf16[1024,1024]{0,1:T(8,128)(2,1)}), bf16[256,1024]{0,1:T(8,128)(2,1)}) %reduce-scatter.15.cloned.1.call-update) | async-done | bytes 524304 | tf_op jit(solution)/shard_map/reduce_scatter | solution.py:207
  919.3 9.9 add_convert_fusion.2
  929.3 35.2 %reduce-scatter.19.cloned.1.call-done = bf16[256,1024]{1,0:T(8,128)(2,1)} async-done(((bf16[1024,1024]{1,0:T(8,128)(2,1)}), bf16[256,1024]{1,0:T(8,128)(2,1)}) %reduce-scatter.19.cloned.1.call-update) | async-done | bytes 524304 | tf_op jit(solution)/shard_map/reduce_scatter | solution.py:322
  964.5 146.0 %reduce-scatter.21.cloned.1.call-done = bf16[256,4096]{1,0:T(8,128)(2,1)} async-done(((bf16[1024,4096]{1,0:T(8,128)(2,1)}), bf16[256,4096]{1,0:T(8,128)(2,1)}) %reduce-scatter.21.cloned.1.call-update) | async-done | bytes 2097168 | tf_op jit(solution)/shard_map/reduce_scatter | solution.py:334
  1110.5 147.5 %reduce-scatter.23.cloned.1.call-done = bf16[1024,1024]{1,0:T(8,128)(2,1)} async-done(((bf16[4096,1024]{1,0:T(8,128)(2,1)}), bf16[1024,1024]{1,0:T(8,128)(2,1)}) %reduce-scatter.23.cloned.1.call-update) | async-done | bytes 2097168 | tf_op jit(solution)/shard_map/reduce_scatter | solution.py:340
  1258.1 113.5 %reduce-scatter.17.cloned.1.call-done = bf16[256,3072]{1,0:T(8,128)(2,1)} async-done(((bf16[1024,3072]{1,0:T(8,128)(2,1)}), bf16[256,3072]{1,0:T(8,128)(2,1)}) %reduce-scatter.17.cloned.1.call-update) | async-done | bytes 1572880 | tf_op jit(solution)/shard_map/reduce_scatter | solution.py:316
  1371.7 10.4 all-gather.7
  1384.6 6.9 fusion.36
  1391.7 6.1 fusion.37
  1405.6 15.8 %all-reduce.10 = (bf16[1024]{0:T(1024)(128)(2,1)S(1)}, bf16[1024]{0:T(1024)(128)(2,1)S(1)}, bf16[3072]{0:T(1024)(128)(2,1)S(1)}, bf16[1024]{0:T(1024)(128)(2,1)S...) all-reduce(bf16[1024]{0:T(1024)(128)(2,1)S(1)} %add_convert_fusion., ...), channel_id=7, replica_groups=mesh['rep'=8,'grp'=4] {'grp'}, use_global_device_ids=true, to_apply=%region_28.29.clone | all-reduce | flops 13312 | bytes 53248
  1421.9 12.9 all-reduce.8
  1443.0 19.7 %all-reduce.13.cloned.1.call-done = (bf16[256,1024]{1,0:T(8,128)(2,1)}, bf16[256,4096]{1,0:T(8,128)(2,1)}, bf16[1024,1024]{1,0:T(8,128)(2,1)}) async-done(((bf16[256,1024]{1,0:T(8,128)(2,1)}, bf16[256,4096]{1,0:T(8,128)(2,1)}, bf16[1024,1024]{1,0:T(8,128)(2,1)}), (bf16[256,1024]{1,0:T(8,128)(2,1)}, bf16[256,4096]{1,0:T(8,128)(2,1)}, bf16[1024,1024]{1,0:T(8,128)(2,1)})) %all-reduce.13.cloned.1.call-update) | async-done | bytes 4718608 | tf_op jit(solution)/shard_map/psum | solution.py:352
  1471.6 65.0 %all-gather.34.cloned.1.call-done = bf16[2048,3072]{1,0:T(8,128)(2,1)} async-done(((bf16[256,3072]{1,0:T(8,128)(2,1)}), bf16[2048,3072]{1,0:T(8,128)(2,1)}) %all-gather.34.cloned.1.call-update) | async-done | bytes 12582928 | tf_op jit(solution)/shard_map/all_gather | solution.py:350
  1536.6 7.3 reduce_sum.360
  (382 shorter events, 150.2 us)
Async XLA Ops:
  7.2 120.6 %all-gather.18.cloned.1.call-start = ((), (), s32[]{:S(2)}) async-start(), calls=%async_computation.8 | async-start | bytes 7864320 | tf_op jit(solution)/shard_map/all_gather | solution.py:280
  7.9 193.0 %all-gather.32.cloned.1.call-start = ((), (), s32[]{:S(2)}) async-start(), calls=%async_computation.15 | async-start | bytes 2621440 | tf_op jit(solution)/shard_map/all_gather | solution.py:89
  23.5 109.2 %copy-start.86 = (f32[4,1,768]{2,1,0:T(1,128)}, f32[4,1,768]{2,1,0:T(1,128)S(1)}, u32[]{:S(2)}) copy-start(f32[4,1,768]{2,1,0:T(1,128)S(1)} %convert_element_type.478) | copy-start | bytes 36868
  36.6 104.3 %copy-start.52 = (f32[4,1,256]{2,1,0:T(1,128)}, f32[4,1,256]{2,1,0:T(1,128)S(1)}, u32[]{:S(2)}) copy-start(f32[4,1,256]{2,1,0:T(1,128)S(1)} %convert_element_type.477) | copy-start | bytes 12292
  45.3 95.6 %copy-start.50 = (f32[4,1,256]{2,1,0:T(1,128)}, f32[4,1,256]{2,1,0:T(1,128)S(1)}, u32[]{:S(2)}) copy-start(f32[4,1,256]{2,1,0:T(1,128)S(1)} %convert_element_type.476) | copy-start | bytes 12292
  46.7 85.9 %copy-start.66 = (f32[256]{0:T(256)}, f32[256]{0:T(256)S(1)}, u32[]{:S(2)}) copy-start(f32[256]{0:T(256)S(1)} %get-tuple-element.142) | copy-start | bytes 3076
  46.8 94.1 %copy-start.64 = (f32[256]{0:T(256)}, f32[256]{0:T(256)S(1)}, u32[]{:S(2)}) copy-start(f32[256]{0:T(256)S(1)} %get-tuple-element.143) | copy-start | bytes 3076
  48.4 84.3 %copy-start.80 = (f32[256]{0:T(256)}, f32[256]{0:T(256)S(1)}, u32[]{:S(2)}) copy-start(f32[256]{0:T(256)S(1)} %add_rsqrt_fusion.1) | copy-start | bytes 3076
  50.1 86.6 %copy-start.60 = (f32[256,32]{0,1:T(8,128)}, f32[256,32]{0,1:T(8,128)S(1)}, u32[]{:S(2)}) copy-start(f32[256,32]{0,1:T(8,128)S(1)} %get-tuple-element.120) | copy-start | bytes 98308
  50.1 103.4 %copy-start.58 = (f32[256,32]{0,1:T(8,128)}, f32[256,32]{0,1:T(8,128)S(1)}, u32[]{:S(2)}) copy-start(f32[256,32]{0,1:T(8,128)S(1)} %get-tuple-element.105) | copy-start | bytes 98308
  137.7 63.2 %copy-start.32 = (bf16[256,16,32]{0,2,1:T(8,128)(2,1)}, bf16[256,16,32]{0,2,1:T(8,128)(2,1)S(1)}, u32[]{:S(2)}) copy-start(bf16[256,16,32]{0,2,1:T(8,128)(2,1)S(1)} %get-tuple-element.81) | copy-start | bytes 786436
  138.6 90.8 %all-gather.30.cloned.1.call-start = ((), (), s32[]{:S(2)}) async-start(), calls=%async_computation.14 | async-start | bytes 2621440 | tf_op jit(solution)/shard_map/all_gather | solution.py:90
  140.8 135.1 %all-gather.20.cloned.1.call-start = ((), (), s32[]{:S(2)}) async-start(), calls=%async_computation.9 | async-start | bytes 2621440 | tf_op jit(solution)/shard_map/all_gather | solution.py:90
  148.3 173.6 %all-gather.24.cloned.1.call-start = ((), (), s32[]{:S(2)}) async-start(), calls=%async_computation.11 | async-start | bytes 2621440 | tf_op jit(solution)/shard_map/all_gather | solution.py:282
  148.9 220.1 %all-gather.22.cloned.1.call-start = ((), (), s32[]{:S(2)}) async-start(), calls=%async_computation.10 | async-start | bytes 2621440 | tf_op jit(solution)/shard_map/all_gather | solution.py:89
  153.6 27.8 %copy-start.96 = (bf16[256]{0:T(256)(128)(2,1)S(1)}, bf16[256]{0:T(256)(128)(2,1)}, u32[]{:S(2)}) copy-start(bf16[256]{0:T(256)(128)(2,1)} %param.24) | copy-start | bytes 1540
  153.6 39.0 %copy-start.97 = (bf16[256]{0:T(256)(128)(2,1)S(1)}, bf16[256]{0:T(256)(128)(2,1)}, u32[]{:S(2)}) copy-start(bf16[256]{0:T(256)(128)(2,1)} %param.23) | copy-start | bytes 1540
  154.7 46.2 %copy-start.34 = (bf16[256,16,32]{0,2,1:T(8,128)(2,1)S(1)}, bf16[256,16,32]{0,2,1:T(8,128)(2,1)}, u32[]{:S(2)}) copy-start(bf16[256,16,32]{0,2,1:T(8,128)(2,1)} %get-tuple-element.82) | copy-start | bytes 786436
  155.6 362.8 %all-gather.26.cloned.1.call-start = ((), (), s32[]{:S(2)}) async-start(), calls=%async_computation.12 | async-start | bytes 10485760 | tf_op jit(solution)/shard_map/all_gather | solution.py:286
  156.3 511.4 %all-gather.28.cloned.1.call-start = ((), (), s32[]{:S(2)}) async-start(), calls=%async_computation.13 | async-start | bytes 10485760 | tf_op jit(solution)/shard_map/all_gather | solution.py:288
  157.1 702.9 %reduce-scatter.13.cloned.1.call-start = ((), (), s32[]{:S(2)}) async-start(), calls=%async_computation.18 | async-start | bytes 2621440 | tf_op jit(solution)/shard_map/reduce_scatter | solution.py:201
  232.3 56.9 %copy-start.9 = (bf16[1024,1024]{0,1:T(8,128)(2,1)}, bf16[1024,1024]{0,1:T(8,128)(2,1)S(1)}, u32[]{:S(2)}) copy-start(bf16[1024,1024]{0,1:T(8,128)(2,1)S(1)} %copy.56) | copy-start | bytes 6291460
  289.2 79.8 %copy-start.36 = (bf16[256,16,32]{0,2,1:T(8,128)(2,1)S(1)}, bf16[256,16,32]{0,2,1:T(8,128)(2,1)}, u32[]{:S(2)}) copy-start(bf16[256,16,32]{0,2,1:T(8,128)(2,1)} %get-tuple-element.77) | copy-start | bytes 786436
  321.8 47.1 %copy-start.38 = (bf16[256,16,32]{0,2,1:T(8,128)(2,1)S(1)}, bf16[256,16,32]{0,2,1:T(8,128)(2,1)}, u32[]{:S(2)}) copy-start(bf16[256,16,32]{0,2,1:T(8,128)(2,1)} %get-tuple-element.78) | copy-start | bytes 786436
  324.5 44.4 %copy-start.83 = (f32[256]{0:T(256)}, f32[256]{0:T(256)S(1)}, u32[]{:S(2)}) copy-start(f32[256]{0:T(256)S(1)} %broadcast_multiply_fusion.8) | copy-start | bytes 3076
  386.7 318.1 %copy-start.87 = (f32[256]{0:T(256)}, f32[256]{0:T(256)S(1)}, u32[]{:S(2)}) copy-start(f32[256]{0:T(256)S(1)} %add_rsqrt_fusion) | copy-start | bytes 3076
  386.8 318.1 %copy-start.71 = (f32[256]{0:T(256)}, f32[256]{0:T(256)S(1)}, u32[]{:S(2)}) copy-start(f32[256]{0:T(256)S(1)} %add_rsqrt_fusion.2) | copy-start | bytes 3076
  518.3 17.1 %copy-start.11 = (f32[256,1024]{1,0:T(8,128)S(1)}, f32[256,1024]{1,0:T(8,128)}, u32[]{:S(2)}) copy-start(f32[256,1024]{1,0:T(8,128)} %copy-done.10) | copy-start | bytes 3145732
  518.3 17.1 %copy-start.77 = (f32[4096]{0:T(1024)S(1)}, f32[4096]{0:T(1024)}, u32[]{:S(2)}) copy-start(f32[4096]{0:T(1024)} %convert_element_type.406) | copy-start | bytes 49156
  518.3 17.1 %copy-start.94 = (bf16[1024,4096]{1,0:T(8,128)(2,1)S(1)}, bf16[1024,4096]{1,0:T(8,128)(2,1)}, u32[]{:S(2)}) copy-start(bf16[1024,4096]{1,0:T(8,128)(2,1)} %all-gather.26.cloned.1.call-done) | copy-start | bytes 25165828
  712.1 17.2 %slice-start.3 = ((s8[16777216]{0:T(1024)(128)(4,1)}), s8[4194304]{0:T(1024)(128)(4,1)S(1)}, s32[]{:S(2)}) async-start(s8[16777216]{0:T(1024)(128)(4,1)} %bitcast.213), calls=%async_computation.29 | async-start | bytes 8388608
  741.7 119.5 %reduce-scatter.9.cloned.1.call-start = ((), (), s32[]{:S(2)}) async-start(), calls=%async_computation.16 | async-start | bytes 2621440 | tf_op jit(solution)/shard_map/reduce_scatter | solution.py:201
  746.5 16.1 %slice-start.5 = ((s8[16777216]{0:T(1024)(128)(4,1)}), s8[4194304]{0:T(1024)(128)(4,1)S(1)}, s32[]{:S(2)}) async-start(s8[16777216]{0:T(1024)(128)(4,1)} %bitcast.215), calls=%async_computation.31 | async-start | bytes 8388608
  746.5 16.1 %slice-start.6 = ((s8[16777216]{0:T(1024)(128)(4,1)}), s8[4194304]{0:T(1024)(128)(4,1)S(1)}, s32[]{:S(2)}) async-start(s8[16777216]{0:T(1024)(128)(4,1)} %bitcast.215), calls=%async_computation.32 | async-start | bytes 8388608
  746.5 17.3 %slice-start.7 = ((s8[16777216]{0:T(1024)(128)(4,1)}), s8[4194304]{0:T(1024)(128)(4,1)S(1)}, s32[]{:S(2)}) async-start(s8[16777216]{0:T(1024)(128)(4,1)} %bitcast.215), calls=%async_computation.33 | async-start | bytes 8388608
  776.1 97.7 %reduce-scatter.11.cloned.1.call-start = ((), (), s32[]{:S(2)}) async-start(), calls=%async_computation.17 | async-start | bytes 2621440 | tf_op jit(solution)/shard_map/reduce_scatter | solution.py:207
  785.6 133.8 %reduce-scatter.15.cloned.1.call-start = ((), (), s32[]{:S(2)}) async-start(), calls=%async_computation.19 | async-start | bytes 2621440 | tf_op jit(solution)/shard_map/reduce_scatter | solution.py:207
  795.3 169.2 %reduce-scatter.19.cloned.1.call-start = ((), (), s32[]{:S(2)}) async-start(), calls=%async_computation.21 | async-start | bytes 2621440 | tf_op jit(solution)/shard_map/reduce_scatter | solution.py:322
  799.5 311.1 %reduce-scatter.21.cloned.1.call-start = ((), (), s32[]{:S(2)}) async-start(), calls=%async_computation.22 | async-start | bytes 10485760 | tf_op jit(solution)/shard_map/reduce_scatter | solution.py:334
  821.6 436.4 %reduce-scatter.23.cloned.1.call-start = ((), (), s32[]{:S(2)}) async-start(), calls=%async_computation.23 | async-start | bytes 10485760 | tf_op jit(solution)/shard_map/reduce_scatter | solution.py:340
  844.7 526.9 %reduce-scatter.17.cloned.1.call-start = ((), (), s32[]{:S(2)}) async-start(), calls=%async_computation.20 | async-start | bytes 7864320 | tf_op jit(solution)/shard_map/reduce_scatter | solution.py:316
  873.8 45.6 %copy-start.67 = (f32[256]{0:T(256)S(1)}, f32[256]{0:T(256)}, u32[]{:S(2)}) copy-start(f32[256]{0:T(256)} %copy-done.66) | copy-start | bytes 3076
  873.8 45.5 %copy-start.81 = (f32[256]{0:T(256)S(1)}, f32[256]{0:T(256)}, u32[]{:S(2)}) copy-start(f32[256]{0:T(256)} %copy-done.80) | copy-start | bytes 3076
  929.2 442.4 %copy-start.98 = (bf16[256]{0:T(256)(128)(2,1)S(1)}, bf16[256]{0:T(256)(128)(2,1)}, u32[]{:S(2)}) copy-start(bf16[256]{0:T(256)(128)(2,1)} %param.28) | copy-start | bytes 1540
  929.2 452.8 %copy-start.99 = (u32[32]{0:T(128)S(1)}, u32[32]{0:T(128)}, u32[]{:S(2)}) copy-start(u32[32]{0:T(128)} %constant.113) | copy-start | bytes 388
  929.3 533.4 %all-reduce.13.cloned.1.call-start = ((), (), s32[]{:S(2)}) async-start(), calls=%async_computation.25 | async-start | bytes 9437184 | tf_op jit(solution)/shard_map/psum | solution.py:352
  1258.0 278.5 %all-gather.34.cloned.1.call-start = ((), (), s32[]{:S(2)}) async-start(), calls=%async_computation.24 | async-start | bytes 14155776 | tf_op jit(solution)/shard_map/all_gather | solution.py:350
  1402.1 37.3 %copy-start.15 = (f32[256,1024]{1,0:T(8,128)S(1)}, f32[256,1024]{1,0:T(8,128)}, u32[]{:S(2)}) copy-start(f32[256,1024]{1,0:T(8,128)} %get-tuple-element.92) | copy-start | bytes 3145732
  (81 other events, 581.8 us)
Sparse Core Ops, SparseCore 0:
  9.6 118.1 all-gather.17
  138.8 44.5 all-gather.31
  185.5 43.8 all-gather.29
  231.4 44.4 all-gather.19
  277.3 44.4 all-gather.23
  323.8 45.0 all-gather.21
  370.5 147.7 all-gather.25
  519.9 147.7 all-gather.27
  741.8 41.7 reduce-scatter.12
  785.8 42.8 reduce-scatter.8
  830.9 42.8 reduce-scatter.10
  876.5 42.8 reduce-scatter.14
  921.6 42.8 reduce-scatter.18
  966.7 143.7 reduce-scatter.20
  1112.7 145.2 reduce-scatter.22
  1260.2 111.4 reduce-scatter.16
  1375.1 87.5 all-reduce.12
  1464.5 72.0 all-gather.33
